TPU v7x, 32 devices: a whole 2x2x4 slice. The times are simulated.
32 devices in a mesh: trc: 4 (over z), lat: 4 (over x, core), lon: 2 (over y).
Axes of the slice: x: 2, y: 2, z: 4, core: 2. Of those that a mesh axis runs over, the one named last changes fastest.
Arguments:
- species_concentrations: float32 [32, 8, 128, 256], P('trc', None, 'lat', 'lon'), may hold values from 0.2 to 4
- zonal_velocity_array: float32 [8, 128, 256], P('trc', 'lat', 'lon'), may hold values from -2.5 to 2.5
- meridional_velocity_array: float32 [8, 128, 256], P('trc', 'lat', 'lon'), may hold values from -2.5 to 2.5
- thermal_anomaly: float32 [8, 128, 256], P('trc', 'lat', 'lon'), may hold values from -6 to 6
- ocean_top_height_grid: float32 [128, 256], P('lat', 'lon'), may hold values from -6 to 6
- water_layer_tally: int32 [128, 256], P('lat', 'lon'), may hold values from 0 to 8
- species_interaction_table: float32 [32, 32], replicated, may hold values from -1 to 1
- species_production_pace: float32 [32], replicated, may hold values from 0.2 to 2
- photon_uptake: float32 [32], replicated, may hold values from 0.01 to 0.1
Outputs:
- updated_tracers: float32 [32, 8, 128, 256], P('trc', None, 'lat', 'lon')
- east_out: float32 [8, 128, 256], P('trc', 'lat', 'lon')
- north_out: float32 [8, 128, 256], P('trc', 'lat', 'lon')
- temperature_out: float32 [8, 128, 256], P('trc', 'lat', 'lon')
- height_out: float32 [128, 256], P('lat', 'lon')
Inputs may be any that keep to these rules, and one draw needn't show every extreme that they name: `water_layer_tally`: the number of wet levels of a column, counted from the surface; cells below it, and whole columns with 0, are land.
All inputs are finite; a program needn't handle non-finite values.
Results may differ from a plain program's by a relative error of at most 0.0003.
Values sent between devices are 32-bit elements; how exact they have to be, the bound alone decides.
No kernel may reach another device: no remote copies, remote signals or barrier semaphores. Data moves between devices by JAX's collectives and lax.ppermute only.
A program may use at most 64 MiB of HBM per device.

v0:
```python
import math
import jax
import jax.numpy as jnp
from jax import lax
from jax.sharding import PartitionSpec as P

HIGHEST = lax.Precision.HIGHEST
TIME_STEP = 0.1
GRAVITY = 1.0
VISCOSITY = 0.2
BOTTOM_DRAG = 0.05
DEPTH_SCALE = 0.5
CORIOLIS_SCALE = 0.5
COLUMN_DEPTH = 2.0
WATER_ABSORB = 0.2
HALF_LIGHT = 0.5
REACT_STEP = 0.1
WARMING_WEIGHT = 1.0


def padded(block, sides, width, periodic):
    for axis, dim in sides:
        count = lax.axis_size(axis)
        forward = [(i, i + 1) for i in range(count - 1)]
        if periodic:
            forward.append((count - 1, 0))
        backward = [(target, source) for source, target in forward]
        low = lax.ppermute(
            lax.slice_in_dim(block, block.shape[dim] - width, None, axis=dim), axis, forward
        )
        high = lax.ppermute(lax.slice_in_dim(block, 0, width, axis=dim), axis, backward)
        block = jnp.concatenate([low, block, high], axis=dim)
    return block


def limited_slope(ahead, behind):
    smaller = jnp.minimum(jnp.abs(ahead), jnp.abs(behind))
    return jnp.where(
        ahead * behind > 0, jnp.where(ahead > 0, smaller, -smaller), jnp.zeros_like(smaller)
    )


def face_flux(before, center, after, beyond, vel_here, vel_next, wet_here, wet_next):
    courant = 0.5 * (vel_here + vel_next) * wet_here * wet_next
    upwind_pos = center + 0.5 * (1.0 - courant) * limited_slope(after - center, center - before)
    upwind_neg = after - 0.5 * (1.0 + courant) * limited_slope(beyond - after, after - center)
    return courant * jnp.where(courant >= 0, upwind_pos, upwind_neg)


def transport(field, flow_east, flow_north, wet):
    free_top_height, width = (field.shape[-2], field.shape[-1])
    rows = slice(2, free_top_height - 2)
    cols = slice(2, width - 2)
    flux_x = face_flux(
        field[..., rows, 0 : width - 3],
        field[..., rows, 1 : width - 2],
        field[..., rows, 2 : width - 1],
        field[..., rows, 3:width],
        flow_east[..., rows, 1 : width - 2],
        flow_east[..., rows, 2 : width - 1],
        wet[..., rows, 1 : width - 2],
        wet[..., rows, 2 : width - 1],
    )
    flux_y = face_flux(
        field[..., 0 : free_top_height - 3, cols],
        field[..., 1 : free_top_height - 2, cols],
        field[..., 2 : free_top_height - 1, cols],
        field[..., 3:free_top_height, cols],
        flow_north[..., 1 : free_top_height - 2, cols],
        flow_north[..., 2 : free_top_height - 1, cols],
        wet[..., 1 : free_top_height - 2, cols],
        wet[..., 2 : free_top_height - 1, cols],
    )
    return (
        field[..., rows, cols]
        - (flux_x[..., 1:] - flux_x[..., :-1])
        - (flux_y[..., 1:, :] - flux_y[..., :-1, :])
    )


def ocean_core(stacked, north, south, east, west, wet, coriolis):
    count = (stacked.shape[0] - 1) // 2
    zonal_flow_value = stacked[:count]
    meridional_flow_value = stacked[count : 2 * count]
    free_top_height = stacked[2 * count]
    lap_east = north[:count] + south[:count] + east[:count] + west[:count] - 4.0 * zonal_flow_value
    lap_north = (
        north[count : 2 * count]
        + south[count : 2 * count]
        + east[count : 2 * count]
        + west[count : 2 * count]
        - 4.0 * meridional_flow_value
    )
    grad_x = 0.5 * (east[2 * count] - west[2 * count])
    grad_y = 0.5 * (north[2 * count] - south[2 * count])
    div_levels = 0.5 * (east[:count] - west[:count]) + 0.5 * (
        north[count : 2 * count] - south[count : 2 * count]
    )
    new_east = wet * (
        zonal_flow_value
        + TIME_STEP
        * (
            coriolis * meridional_flow_value
            - GRAVITY * grad_x
            + VISCOSITY * lap_east
            - BOTTOM_DRAG * zonal_flow_value
        )
    )
    new_north = wet * (
        meridional_flow_value
        + TIME_STEP
        * (
            -coriolis * zonal_flow_value
            - GRAVITY * grad_y
            + VISCOSITY * lap_north
            - BOTTOM_DRAG * meridional_flow_value
        )
    )
    return (new_east, new_north, free_top_height, jnp.sum(div_levels, 0))


def ocean_step(zonal_flow_value, meridional_flow_value, free_top_height, wet, coriolis):
    stacked = jnp.concatenate([zonal_flow_value, meridional_flow_value, free_top_height[None]], 0)
    by_lat = padded(stacked, (("lat", 1),), 1, False)
    by_lon = padded(stacked, (("lon", 2),), 1, True)
    new_east, new_north, free_top_height, partial_div = ocean_core(
        stacked,
        by_lat[:, 2:, :],
        by_lat[:, :-2, :],
        by_lon[:, :, 2:],
        by_lon[:, :, :-2],
        wet,
        coriolis,
    )
    divergence = lax.psum(partial_div, "trc")
    return (new_east, new_north, free_top_height - TIME_STEP * DEPTH_SCALE * divergence)


def widen_flow(flow, width):
    rows_ext = padded(flow, (("lat", 2),), width, False)
    return padded(rows_ext, (("lon", 3),), width, True)


def widen_tracers(field, width):
    rows_ext = padded(field, (("lat", 2),), width, False)
    return padded(rows_ext, (("lon", 3),), width, True)


def light_profile(absorbed, wet, surface):
    levels = absorbed.shape[0]
    layer = COLUMN_DEPTH / levels * (WATER_ABSORB + absorbed) * wet
    above = jnp.cumsum(layer, 0) - layer
    top_light = surface[None, :, None] * jnp.exp(-above)
    return (top_light * (1.0 - jnp.exp(-layer)), top_light / (top_light + HALF_LIGHT))


def body(
    species_concentrations,
    zonal_velocity_array,
    meridional_velocity_array,
    thermal_anomaly,
    ocean_top_height_grid,
    water_layer_tally,
    species_interaction_table,
    species_production_pace,
    photon_uptake,
):
    tracer_count, levels, lat_rows, lon_cols = species_concentrations.shape
    own_levels = zonal_velocity_array.shape[0]
    trc_place = lax.axis_index("trc")
    lat_total = lat_rows * lax.axis_size("lat")
    lat_global = (lax.axis_index("lat") * lat_rows + jnp.arange(lat_rows)).astype(jnp.float32)
    angle = math.pi * ((lat_global + 0.5) / lat_total - 0.5)
    coriolis = CORIOLIS_SCALE * jnp.sin(angle)[:, None]
    surface = 1.0 + jnp.cos(angle)
    depth_index = jnp.arange(levels)
    wet_all = (depth_index[:, None, None] < water_layer_tally[None]).astype(jnp.float32)
    wet_own = lax.dynamic_slice_in_dim(wet_all, trc_place * own_levels, own_levels, 0)
    east_start = wet_own * zonal_velocity_array
    north_start = wet_own * meridional_velocity_array
    zonal_flow_value, meridional_flow_value, free_top_height = (
        east_start,
        north_start,
        ocean_top_height_grid,
    )
    for substep in range(2):
        zonal_flow_value, meridional_flow_value, free_top_height = ocean_step(
            zonal_flow_value, meridional_flow_value, free_top_height, wet_own, coriolis
        )
    velocity = lax.all_gather(jnp.stack([east_start, north_start]), "trc", axis=1, tiled=True)
    flow = jnp.concatenate([velocity, wet_all[None]], 0)
    flow_ext = widen_flow(flow, 4)
    first = transport(
        widen_tracers(species_concentrations, 4), flow_ext[0], flow_ext[1], flow_ext[2]
    )
    inner = flow_ext[:, :, 2:-2, 2:-2]
    moved = transport(first, inner[0], inner[1], inner[2])
    share = lat_rows // lax.axis_size("trc")
    columns = lax.all_to_all(moved, "trc", split_axis=2, concat_axis=0, tiled=True)
    wet_cols = lax.dynamic_slice_in_dim(wet_all, trc_place * share, share, 1)
    surface_cols = lax.dynamic_slice_in_dim(surface, trc_place * share, share, 0)
    absorbed = jnp.einsum("n,nkyx->kyx", photon_uptake, jnp.abs(columns), precision=HIGHEST)
    solar_warming, light_factor = light_profile(absorbed, wet_cols, surface_cols)
    mixed = jnp.einsum("mn,nkyx->mkyx", species_interaction_table, columns, precision=HIGHEST)
    species_postchemistry = columns + wet_cols * REACT_STEP * (
        mixed + species_production_pace[:, None, None, None] * light_factor * columns
    )
    updated_tracers = lax.all_to_all(
        species_postchemistry, "trc", split_axis=0, concat_axis=2, tiled=True
    )
    pointwise_warming_pace = lax.all_to_all(
        solar_warming, "trc", split_axis=0, concat_axis=1, tiled=True
    )
    return (
        updated_tracers,
        zonal_flow_value,
        meridional_flow_value,
        thermal_anomaly + WARMING_WEIGHT * pointwise_warming_pace,
        free_top_height,
    )


def solution(mesh):
    return jax.shard_map(
        body,
        mesh=mesh,
        in_specs=(
            P("trc", None, "lat", "lon"),
            P("trc", "lat", "lon"),
            P("trc", "lat", "lon"),
            P("trc", "lat", "lon"),
            P("lat", "lon"),
            P("lat", "lon"),
            P(),
            P(),
            P(),
        ),
        out_specs=(
            P("trc", None, "lat", "lon"),
            P("trc", "lat", "lon"),
            P("trc", "lat", "lon"),
            P("trc", "lat", "lon"),
            P("lat", "lon"),
        ),
        check_vma=False,
    )
```

profile of v0, /device:TPU:0, one launch (start us, length us, event | category | flops | bytes accessed | tf_op | source)
XLA Modules:
  0.0 207.8 jit_solution(16878511505992361957)
XLA Ops:
  3.0 15.7 %all_gather.3 = f32[2,8,32,128]{3,2,0,1:T(8,128)S(1)} all-gather(f32[2,2,32,128]{3,2,0,1:T(8,128)S(1)} %pad_maximum_fusion.8), channel_id=1, replica_groups=mesh['trc'=4,'lat'=4,'lon'=2] {'trc'}, dimensions={1}, use_global_device_ids=true | all-gather | bytes 327680 | tf_op jit(solution)/shard_map/all_gather | solution.py:190
  18.9 1.3 collective-permute-start.5
  20.2 3.0 %collective-permute-start.4 = (f32[3,8,4,128]{3,1,2,0:T(8,128)S(1)}, f32[3,8,4,128]{3,1,2,0:T(8,128)S(1)}, u32[]{:S(2)}, u32[]{:S(2)}) collective-permute-start(f32[3,8,4,128]{3,1,2,0:T(8,128)S(1)} %get-tuple-element.30), channel_id=1, source_target_pairs={{0,2},{2,4},{4,6},{1,3},{3,5},{5,7},{8,10},{10,12},{12,14},{9,11},... | collective-permute-start | bytes 147464 | tf_op jit(solution)/shard_map/ppermute | solution.py:28
  25.0 1.5 collective-permute-start.7
  27.8 1.3 collective-permute-start.1
  29.7 4.0 %collective-permute-start = (f32[8,8,4,128]{3,1,2,0:T(8,128)}, f32[8,8,4,128]{3,1,2,0:T(8,128)}, u32[]{:S(2)}, u32[]{:S(2)}) collective-permute-start(f32[8,8,4,128]{3,1,2,0:T(8,128)} %copy.159), channel_id=1, source_target_pairs={{0,2},{2,4},{4,6},{1,3},{3,5},{5,7},{8,10},{10,12},{12,14},{9,11},... | collective-permute-start | bytes 393224 | tf_op jit(solution)/shard_map/ppermute | solution.py:28
  33.7 2.7 %copy.131 = f32[8,8,32,128]{2,1,3,0:T(8,128)} copy(f32[8,8,32,128]{3,2,1,0:T(8,128)S(1)} %copy-done.8) | data formatting | bytes 2097152 | tf_op args[0]
  36.4 2.5 %collective-permute-done.7 = f32[3,8,40,4]{3,1,2,0:T(8,128)S(1)} collective-permute-done((f32[3,8,40,4]{3,1,2,0:T(8,128)}, f32[3,8,40,4]{3,1,2,0:T(8,128)S(1)}, u32[]{:S(2)}, u32[]{:S(2)}) %collective-permute-start.7) | collective-permute-done | bytes 15392 | tf_op jit(solution)/shard_map/ppermute | solution.py:31
  38.9 10.5 %collective-permute-done.6 = f32[3,8,40,4]{3,1,2,0:T(8,128)S(1)} collective-permute-done((f32[3,8,40,4]{3,1,2,0:T(8,128)S(1)}, f32[3,8,40,4]{3,1,2,0:T(8,128)S(1)}, u32[]{:S(2)}, u32[]{:S(2)}) %collective-permute-start.6) | collective-permute-done | bytes 15392 | tf_op jit(solution)/shard_map/ppermute | solution.py:28
  55.2 3.6 %copy.132 = f32[8,8,4,128]{2,1,3,0:T(8,128)} copy(f32[8,8,4,128]{3,1,2,0:T(8,128)} %collective-permute-done.1) | data formatting | bytes 262144 | tf_op jit(solution)/shard_map/ppermute | solution.py:31
  58.8 3.5 %copy.130 = f32[8,8,4,128]{2,1,3,0:T(8,128)} copy(f32[8,8,4,128]{3,1,2,0:T(8,128)} %collective-permute-done) | data formatting | bytes 262144 | tf_op jit(solution)/shard_map/ppermute | solution.py:28
  62.3 2.1 %pad_maximum_fusion.5 = (f32[8,8,40,4]{2,1,3,0:T(8,128)}, f32[8,8,40,4]{2,1,3,0:T(8,128)}) fusion(f32[8,8,4,128]{2,1,3,0:T(8,128)} %copy.132, f32[8,8,32,128]{2,1,3,0:T(8,128)} %copy.131, f32[8,8,4,128]{2,1,3,0:T(8,128)} %copy.130), kind=kLoop, calls=%fused_computation.120 | loop fusion | flops 40960 | bytes 1392640 | tf_op jit(solution)/shard_map/slice | solution.py:29
  64.4 1.5 collective-permute-start.3
  69.0 1.2 copy.143
  70.6 1.2 copy.141
  72.3 1.4 copy.138
  73.6 1.4 copy.137
  75.0 1.3 copy.136
  76.3 1.9 copy.150
  80.4 2.1 %copy.146 = f32[8,32,129]{1,0,2:T(8,128)} copy(f32[8,32,129]{2,0,1:T(8,128)} %get-tuple-element.37) | data formatting | bytes 264192 | tf_op jit(solution)/shard_map/mul | solution.py:46
  82.5 2.1 %copy.145 = f32[8,32,129]{1,0,2:T(8,128)} copy(f32[8,32,129]{2,0,1:T(8,128)} %get-tuple-element.36) | data formatting | bytes 264192 | tf_op jit(solution)/shard_map/mul | solution.py:45
  84.6 1.2 copy.144
  85.9 6.0 %pad_maximum_fusion = f32[8,8,40,136]{2,1,3,0:T(8,128)S(1)} fusion(f32[8,8,40,4]{2,1,3,0:T(8,128)} %collective-permute-done.3, f32[8,8,4,128]{2,1,3,0:T(8,128)} %copy.132, f32[8,8,32,128]{2,1,3,0:T(8,128)} %copy.131, f32[8,8,4,128]{2,1,3,0:T(8,128)} %copy.130, f32[8,8,40,4]{2,1,3,0:T(8,128)} %collective-permute-done.2), kind=kLoop, calls=%fused_computation.8 | loop fusion | flops 1392640 | bytes 2785280 | tf_op jit(solution)/shard_map/concatenate | solution.py:32
  91.8 4.3 %fusion.12 = f32[8,8,37,132]{2,1,3,0:T(8,128)S(1)} fusion(f32[8,8,40,136]{2,1,3,0:T(8,128)S(1)} %pad_maximum_fusion, f32[8,37,132]{1,0,2:T(8,128)S(1)} %copy.142, f32[8,37,132]{1,0,2:T(8,128)S(1)} %copy-done.1, f32[8,37,132]{1,0,2:T(8,128)S(1)} %copy.139, pred[8,37,132]{1,0,2:T(8,128)(4,1)S(1)} %copy.140), kind=kLoop, calls=%fused_computation.26 | loop fusion | flops 8126976 | bytes 6759456 | tf_op jit(solution)/shard_map/mul | solution.py:47
  96.1 5.1 %fusion.4 = f32[8,8,36,133]{2,1,3,0:T(8,128)S(1)} fusion(f32[8,8,40,136]{2,1,3,0:T(8,128)S(1)} %pad_maximum_fusion, f32[8,36,133]{1,0,2:T(8,128)S(1)} %copy.138, f32[8,36,133]{1,0,2:T(8,128)S(1)} %copy.137, f32[8,36,133]{1,0,2:T(8,128)S(1)} %copy.135, pred[8,36,133]{1,0,2:T(8,128)(4,1)S(1)} %copy.136), kind=kLoop, calls=%fused_computation.13 | loop fusion | flops 7967232 | bytes 6626592 | tf_op jit(solution)/shard_map/mul | solution.py:47
  101.3 2.6 %fusion.16 = f32[8,8,36,132]{2,1,3,0:T(8,128)S(1)} fusion(f32[8,8,37,132]{2,1,3,0:T(8,128)S(1)} %fusion.12, f32[8,8,36,133]{2,1,3,0:T(8,128)S(1)} %fusion.4, f32[8,8,40,136]{2,1,3,0:T(8,128)S(1)} %pad_maximum_fusion), kind=kLoop, calls=%fused_computation.31 | loop fusion | flops 1216512 | bytes 7299072 | tf_op jit(solution)/shard_map/sub | solution.py:75
  103.9 4.2 %fusion.30 = f32[8,8,33,128]{2,1,3,0:T(8,128)S(1)} fusion(f32[8,8,36,132]{2,1,3,0:T(8,128)S(1)} %fusion.16, f32[8,33,128]{1,0,2:T(8,128)S(1)} %copy-done.6, f32[8,33,128]{1,0,2:T(8,128)S(1)} %copy-done.7, f32[8,33,128]{1,0,2:T(8,128)S(1)} %copy-done.5, pred[8,33,128]{1,0,2:T(8,128)(4,1)S(1)} %copy.148), kind=kLoop, calls=%fused_computation.56 | loop fusion | flops 7028736 | bytes 5846016 | tf_op jit(solution)/shard_map/mul | solution.py:47
  108.1 4.7 %fusion.22 = f32[8,8,32,129]{2,1,3,0:T(8,128)S(1)} fusion(f32[8,8,36,132]{2,1,3,0:T(8,128)S(1)} %fusion.16, f32[8,32,129]{1,0,2:T(8,128)S(1)} %copy-done.3, f32[8,32,129]{1,0,2:T(8,128)S(1)} %copy-done.4, f32[8,32,129]{1,0,2:T(8,128)S(1)} %copy-done.2, pred[8,32,129]{1,0,2:T(8,128)(4,1)S(1)} %copy.144), kind=kLoop, calls=%fused_computation.43 | loop fusion | flops 6868992 | bytes 5713152 | tf_op jit(solution)/shard_map/mul | solution.py:47
  112.9 3.8 %fusion.34 = f32[8,8,32,128]{2,1,3,0:T(8,128)} fusion(f32[8,8,33,128]{2,1,3,0:T(8,128)S(1)} %fusion.30, f32[8,8,32,129]{2,1,3,0:T(8,128)S(1)} %fusion.22, f32[8,8,36,132]{2,1,3,0:T(8,128)S(1)} %fusion.16), kind=kLoop, calls=%fused_computation.61 | loop fusion | flops 1048576 | bytes 6291456 | tf_op jit(solution)/shard_map/sub | solution.py:75
  116.6 3.9 %copy.151 = f32[8,8,32,128]{3,1,0,2:T(8,128)} copy(f32[8,8,32,128]{2,1,3,0:T(8,128)} %fusion.34) | data formatting | bytes 2097152 | tf_op jit(solution)/shard_map/sub | solution.py:75
  120.6 5.2 %all-to-all-start = ((f32[8,8,32,128]{3,1,0,2:T(8,128)}), f32[8,8,32,128]{3,1,0,2:T(8,128)S(1)}, u32[]{:S(2)}, u32[]{:S(2)}) async-start(f32[8,8,32,128]{3,1,0,2:T(8,128)} %copy.151), calls=%async_computation | async-start | bytes 2097152 | tf_op jit(solution)/shard_map/all_to_all | solution.py:199
  125.8 1.3 collective-permute-start.11
  127.1 1.3 collective-permute-start.10
  128.5 1.6 collective-permute-start.9
  130.8 2.2 %collective-permute-done.9 = f32[5,32,1]{2,1,0:T(8,128)S(1)} collective-permute-done((f32[5,32,1]{2,1,0:T(8,128)S(1)}, f32[5,32,1]{2,1,0:T(8,128)S(1)}, u32[]{:S(2)}, u32[]{:S(2)}) %collective-permute-start.9) | collective-permute-done | bytes 672 | tf_op jit(solution)/shard_map/ppermute | solution.py:28
  133.0 2.2 %collective-permute-done.8 = f32[5,32,1]{2,1,0:T(8,128)S(1)} collective-permute-done((f32[5,32,1]{2,1,0:T(8,128)S(1)}, f32[5,32,1]{2,1,0:T(8,128)S(1)}, u32[]{:S(2)}, u32[]{:S(2)}) %collective-permute-start.8) | collective-permute-done | bytes 672 | tf_op jit(solution)/shard_map/ppermute | solution.py:31
  135.4 24.5 %psum.14 = f32[32,128]{1,0:T(8,128)S(1)} all-reduce(f32[32,128]{1,0:T(8,128)S(1)} %multiply_reduce_fusion.1), channel_id=1, replica_groups=mesh['trc'=4,'lat'=4,'lon'=2] {'trc'}, use_global_device_ids=true, to_apply=%region_2.0 | all-reduce | flops 4096 | bytes 32768 | tf_op jit(solution)/shard_map/psum | solution.py:135
  161.7 3.4 %all-to-all-start.2 = ((f32[8,8,128]{2,1,0:T(8,128)}), f32[8,8,128]{2,1,0:T(8,128)S(1)}, u32[]{:S(2)}, u32[]{:S(2)}) async-start(f32[8,8,128]{2,1,0:T(8,128)} %get-tuple-element.40), calls=%async_computation.2 | async-start | bytes 65536 | tf_op jit(solution)/shard_map/all_to_all | solution.py:211
  165.1 1.3 fusion.38
  166.4 1.6 copy.153
  168.0 2.7 %all-to-all-done.2 = f32[8,8,128]{2,1,0:T(8,128)S(1)} async-done(((f32[8,8,128]{2,1,0:T(8,128)}), f32[8,8,128]{2,1,0:T(8,128)S(1)}, u32[]{:S(2)}, u32[]{:S(2)}) %all-to-all-start.2) | async-done | bytes 32800 | tf_op jit(solution)/shard_map/all_to_all | solution.py:211
  170.7 3.5 %all-to-all-start.1 = ((f32[32,8,8,128]{3,2,1,0:T(8,128)}), f32[32,8,8,128]{3,2,1,0:T(8,128)S(1)}, u32[]{:S(2)}, u32[]{:S(2)}) async-start(f32[32,8,8,128]{3,2,1,0:T(8,128)} %copy.153), calls=%async_computation.1 | async-start | bytes 2097152 | tf_op jit(solution)/shard_map/all_to_all | solution.py:208
  174.3 1.3 collective-permute-start.15
  175.6 1.3 collective-permute-start.14
  177.0 1.6 collective-permute-start.13
  179.1 3.1 %collective-permute-done.13 = f32[5,32,1]{2,1,0:T(8,128)S(1)} collective-permute-done((f32[5,32,1]{2,1,0:T(8,128)S(1)}, f32[5,32,1]{2,1,0:T(8,128)S(1)}, u32[]{:S(2)}, u32[]{:S(2)}) %collective-permute-start.13) | collective-permute-done | bytes 672 | tf_op jit(solution)/shard_map/ppermute | solution.py:28
  182.2 1.8 collective-permute-done.12
  184.1 19.9 %psum.15 = f32[32,128]{1,0:T(8,128)S(1)} all-reduce(f32[32,128]{1,0:T(8,128)S(1)} %multiply_reduce_fusion), channel_id=1, replica_groups=mesh['trc'=4,'lat'=4,'lon'=2] {'trc'}, use_global_device_ids=true, to_apply=%region_4.5 | all-reduce | flops 4096 | bytes 32768 | tf_op jit(solution)/shard_map/psum | solution.py:135
  (96 shorter events, 25.3 us)
Async XLA Ops:
  0.6 164.5 %copy-start = (f32[32,32]{1,0:T(8,128)S(1)}, f32[32,32]{1,0:T(8,128)}, u32[]{:S(2)}) copy-start(f32[32,32]{1,0:T(8,128)} %param.15) | copy-start | bytes 12292
  0.6 26.4 %copy-start.8 = (f32[8,8,32,128]{3,2,1,0:T(8,128)S(1)}, f32[8,8,32,128]{3,2,1,0:T(8,128)}, u32[]{:S(2)}) copy-start(f32[8,8,32,128]{3,2,1,0:T(8,128)} %param.9) | copy-start | bytes 3145732
  18.9 4.3 %collective-permute-start.5 = (f32[3,8,4,128]{3,1,2,0:T(8,128)S(1)}, f32[3,8,4,128]{3,1,2,0:T(8,128)S(1)}, u32[]{:S(2)}, u32[]{:S(2)}) collective-permute-start(f32[3,8,4,128]{3,1,2,0:T(8,128)S(1)} %get-tuple-element.31), channel_id=1, source_target_pairs={{2,0},{4,2},{6,4},{3,1},{5,3},{7,5},{10,8},{12,10},{14,12},{11,9},... | collective-permute-start | bytes 147464 | tf_op jit(solution)/shard_map/ppermute | solution.py:31
  20.2 3.9 %collective-permute-start.4 = (f32[3,8,4,128]{3,1,2,0:T(8,128)S(1)}, f32[3,8,4,128]{3,1,2,0:T(8,128)S(1)}, u32[]{:S(2)}, u32[]{:S(2)}) collective-permute-start(f32[3,8,4,128]{3,1,2,0:T(8,128)S(1)} %get-tuple-element.30), channel_id=1, source_target_pairs={{0,2},{2,4},{4,6},{1,3},{3,5},{5,7},{8,10},{10,12},{12,14},{9,11},... | collective-permute-start | bytes 147464 | tf_op jit(solution)/shard_map/ppermute | solution.py:28
  25.0 13.9 %collective-permute-start.7 = (f32[3,8,40,4]{3,1,2,0:T(8,128)}, f32[3,8,40,4]{3,1,2,0:T(8,128)S(1)}, u32[]{:S(2)}, u32[]{:S(2)}) collective-permute-start(f32[3,8,40,4]{3,1,2,0:T(8,128)} %get-tuple-element.29), channel_id=1, source_target_pairs={{1,0},{0,1},{3,2},{2,3},{5,4},{4,5},{7,6},{6,7},{9,8},{8,9},{11,10... | collective-permute-start | bytes 46088 | tf_op jit(solution)/shard_map/ppermute | solution.py:31
  26.5 22.9 %collective-permute-start.6 = (f32[3,8,40,4]{3,1,2,0:T(8,128)S(1)}, f32[3,8,40,4]{3,1,2,0:T(8,128)S(1)}, u32[]{:S(2)}, u32[]{:S(2)}) collective-permute-start(f32[3,8,40,4]{3,1,2,0:T(8,128)S(1)} %get-tuple-element.28), channel_id=1, source_target_pairs={{0,1},{1,0},{2,3},{3,2},{4,5},{5,4},{6,7},{7,6},{8,9},{9,8},{10,11... | collective-permute-start | bytes 46088 | tf_op jit(solution)/shard_map/ppermute | solution.py:28
  27.8 27.4 %collective-permute-start.1 = (f32[8,8,4,128]{3,1,2,0:T(8,128)}, f32[8,8,4,128]{3,1,2,0:T(8,128)}, u32[]{:S(2)}, u32[]{:S(2)}) collective-permute-start(f32[8,8,4,128]{3,1,2,0:T(8,128)} %copy.160), channel_id=1, source_target_pairs={{2,0},{4,2},{6,4},{3,1},{5,3},{7,5},{10,8},{12,10},{14,12},{11,9},... | collective-permute-start | bytes 393224 | tf_op jit(solution)/shard_map/ppermute | solution.py:31
  29.7 29.1 %collective-permute-start = (f32[8,8,4,128]{3,1,2,0:T(8,128)}, f32[8,8,4,128]{3,1,2,0:T(8,128)}, u32[]{:S(2)}, u32[]{:S(2)}) collective-permute-start(f32[8,8,4,128]{3,1,2,0:T(8,128)} %copy.159), channel_id=1, source_target_pairs={{0,2},{2,4},{4,6},{1,3},{3,5},{5,7},{8,10},{10,12},{12,14},{9,11},... | collective-permute-start | bytes 393224 | tf_op jit(solution)/shard_map/ppermute | solution.py:28
  64.4 21.4 %collective-permute-start.3 = (f32[8,8,40,4]{2,1,3,0:T(8,128)}, f32[8,8,40,4]{2,1,3,0:T(8,128)}, u32[]{:S(2)}, u32[]{:S(2)}) collective-permute-start(f32[8,8,40,4]{2,1,3,0:T(8,128)} %get-tuple-element.19), channel_id=1, source_target_pairs={{1,0},{0,1},{3,2},{2,3},{5,4},{4,5},{7,6},{6,7},{9,8},{8,9},{11,10... | collective-permute-start | bytes 122888 | tf_op jit(solution)/shard_map/ppermute | solution.py:31
  65.9 19.9 %collective-permute-start.2 = (f32[8,8,40,4]{2,1,3,0:T(8,128)}, f32[8,8,40,4]{2,1,3,0:T(8,128)}, u32[]{:S(2)}, u32[]{:S(2)}) collective-permute-start(f32[8,8,40,4]{2,1,3,0:T(8,128)} %get-tuple-element.18), channel_id=1, source_target_pairs={{0,1},{1,0},{2,3},{3,2},{4,5},{5,4},{6,7},{7,6},{8,9},{9,8},{10,11... | collective-permute-start | bytes 122888 | tf_op jit(solution)/shard_map/ppermute | solution.py:28
  70.2 8.0 %copy-start.10 = (f32[8,33,128]{2,0,1:T(8,128)S(1)}, f32[8,33,128]{2,0,1:T(8,128)}, u32[]{:S(2)}) copy-start(f32[8,33,128]{2,0,1:T(8,128)} %get-tuple-element.38) | copy-start | bytes 405508
  85.8 6.0 %copy-start.1 = (f32[8,37,132]{1,0,2:T(8,128)S(1)}, f32[8,37,132]{1,0,2:T(8,128)}, u32[]{:S(2)}) copy-start(f32[8,37,132]{1,0,2:T(8,128)} %copy.141) | copy-start | bytes 468868
  101.2 2.6 %copy-start.5 = (f32[8,33,128]{1,0,2:T(8,128)S(1)}, f32[8,33,128]{1,0,2:T(8,128)}, u32[]{:S(2)}) copy-start(f32[8,33,128]{1,0,2:T(8,128)} %copy.147) | copy-start | bytes 405508
  101.3 2.6 %copy-start.6 = (f32[8,33,128]{1,0,2:T(8,128)S(1)}, f32[8,33,128]{1,0,2:T(8,128)}, u32[]{:S(2)}) copy-start(f32[8,33,128]{1,0,2:T(8,128)} %copy.150) | copy-start | bytes 405508
  101.3 2.6 %copy-start.7 = (f32[8,33,128]{1,0,2:T(8,128)S(1)}, f32[8,33,128]{1,0,2:T(8,128)}, u32[]{:S(2)}) copy-start(f32[8,33,128]{1,0,2:T(8,128)} %copy.149) | copy-start | bytes 405508
  103.9 4.3 %copy-start.2 = (f32[8,32,129]{1,0,2:T(8,128)S(1)}, f32[8,32,129]{1,0,2:T(8,128)}, u32[]{:S(2)}) copy-start(f32[8,32,129]{1,0,2:T(8,128)} %copy.143) | copy-start | bytes 396292
  103.9 4.3 %copy-start.3 = (f32[8,32,129]{1,0,2:T(8,128)S(1)}, f32[8,32,129]{1,0,2:T(8,128)}, u32[]{:S(2)}) copy-start(f32[8,32,129]{1,0,2:T(8,128)} %copy.146) | copy-start | bytes 396292
  103.9 4.3 %copy-start.4 = (f32[8,32,129]{1,0,2:T(8,128)S(1)}, f32[8,32,129]{1,0,2:T(8,128)}, u32[]{:S(2)}) copy-start(f32[8,32,129]{1,0,2:T(8,128)} %copy.145) | copy-start | bytes 396292
  116.6 9.1 %copy-start.9 = (f32[32,128]{1,0:T(8,128)S(1)}, f32[32,128]{1,0:T(8,128)}, u32[]{:S(2)}) copy-start(f32[32,128]{1,0:T(8,128)} %param.13) | copy-start | bytes 49156
  116.6 43.5 %copy-start.12 = (f32[32]{0:T(128)S(1)}, f32[32]{0:T(128)}, u32[]{:S(2)}) copy-start(f32[32]{0:T(128)} %param.17) | copy-start | bytes 388
  116.6 48.5 %copy-start.13 = (f32[32]{0:T(128)S(1)}, f32[32]{0:T(128)}, u32[]{:S(2)}) copy-start(f32[32]{0:T(128)} %param.16) | copy-start | bytes 388
  120.6 39.6 %all-to-all-start = ((f32[8,8,32,128]{3,1,0,2:T(8,128)}), f32[8,8,32,128]{3,1,0,2:T(8,128)S(1)}, u32[]{:S(2)}, u32[]{:S(2)}) async-start(f32[8,8,32,128]{3,1,0,2:T(8,128)} %copy.151), calls=%async_computation | async-start | bytes 2097152 | tf_op jit(solution)/shard_map/all_to_all | solution.py:199
  125.8 9.5 %collective-permute-start.11 = (f32[5,1,128]{2,1,0:T(1,128)S(1)}, f32[5,1,128]{2,1,0:T(1,128)S(1)}, u32[]{:S(2)}, u32[]{:S(2)}) collective-permute-start(f32[5,1,128]{2,1,0:T(1,128)S(1)} %get-tuple-element.55), channel_id=1, source_target_pairs={{0,2},{2,4},{4,6},{1,3},{3,5},{5,7},{8,10},{10,12},{12,14},{9,11},... | collective-permute-start | bytes 7688 | tf_op jit(solution)/shard_map/ppermute | solution.py:28
  127.1 8.2 %collective-permute-start.10 = (f32[5,1,128]{2,1,0:T(1,128)S(1)}, f32[5,1,128]{2,1,0:T(1,128)S(1)}, u32[]{:S(2)}, u32[]{:S(2)}) collective-permute-start(f32[5,1,128]{2,1,0:T(1,128)S(1)} %get-tuple-element.54), channel_id=1, source_target_pairs={{2,0},{4,2},{6,4},{3,1},{5,3},{7,5},{10,8},{12,10},{14,12},{11,9},... | collective-permute-start | bytes 7688 | tf_op jit(solution)/shard_map/ppermute | solution.py:31
  128.5 4.5 %collective-permute-start.9 = (f32[5,32,1]{2,1,0:T(8,128)S(1)}, f32[5,32,1]{2,1,0:T(8,128)S(1)}, u32[]{:S(2)}, u32[]{:S(2)}) collective-permute-start(f32[5,32,1]{2,1,0:T(8,128)S(1)} %get-tuple-element.53), channel_id=1, source_target_pairs={{0,1},{1,0},{2,3},{3,2},{4,5},{5,4},{6,7},{7,6},{8,9},{9,8},{10,11... | collective-permute-start | bytes 1928 | tf_op jit(solution)/shard_map/ppermute | solution.py:28
  130.1 5.2 %collective-permute-start.8 = (f32[5,32,1]{2,1,0:T(8,128)S(1)}, f32[5,32,1]{2,1,0:T(8,128)S(1)}, u32[]{:S(2)}, u32[]{:S(2)}) collective-permute-start(f32[5,32,1]{2,1,0:T(8,128)S(1)} %get-tuple-element.52), channel_id=1, source_target_pairs={{1,0},{0,1},{3,2},{2,3},{5,4},{4,5},{7,6},{6,7},{9,8},{8,9},{11,10... | collective-permute-start | bytes 1928 | tf_op jit(solution)/shard_map/ppermute | solution.py:31
  161.7 44.4 %copy-start.11 = (f32[2,32,128]{2,1,0:T(8,128)S(1)}, f32[2,32,128]{2,1,0:T(8,128)}, u32[]{:S(2)}) copy-start(f32[2,32,128]{2,1,0:T(8,128)} %param.12) | copy-start | bytes 98308
  161.7 9.0 %all-to-all-start.2 = ((f32[8,8,128]{2,1,0:T(8,128)}), f32[8,8,128]{2,1,0:T(8,128)S(1)}, u32[]{:S(2)}, u32[]{:S(2)}) async-start(f32[8,8,128]{2,1,0:T(8,128)} %get-tuple-element.40), calls=%async_computation.2 | async-start | bytes 65536 | tf_op jit(solution)/shard_map/all_to_all | solution.py:211
  170.7 36.0 %all-to-all-start.1 = ((f32[32,8,8,128]{3,2,1,0:T(8,128)}), f32[32,8,8,128]{3,2,1,0:T(8,128)S(1)}, u32[]{:S(2)}, u32[]{:S(2)}) async-start(f32[32,8,8,128]{3,2,1,0:T(8,128)} %copy.153), calls=%async_computation.1 | async-start | bytes 2097152 | tf_op jit(solution)/shard_map/all_to_all | solution.py:208
  174.3 9.7 %collective-permute-start.15 = (f32[5,1,128]{2,1,0:T(1,128)S(1)}, f32[5,1,128]{2,1,0:T(1,128)S(1)}, u32[]{:S(2)}, u32[]{:S(2)}) collective-permute-start(f32[5,1,128]{2,1,0:T(1,128)S(1)} %get-tuple-element.49), channel_id=1, source_target_pairs={{0,2},{2,4},{4,6},{1,3},{3,5},{5,7},{8,10},{10,12},{12,14},{9,11},... | collective-permute-start | bytes 7688 | tf_op jit(solution)/shard_map/ppermute | solution.py:28
  175.6 8.4 %collective-permute-start.14 = (f32[5,1,128]{2,1,0:T(1,128)S(1)}, f32[5,1,128]{2,1,0:T(1,128)S(1)}, u32[]{:S(2)}, u32[]{:S(2)}) collective-permute-start(f32[5,1,128]{2,1,0:T(1,128)S(1)} %get-tuple-element.48), channel_id=1, source_target_pairs={{2,0},{4,2},{6,4},{3,1},{5,3},{7,5},{10,8},{12,10},{14,12},{11,9},... | collective-permute-start | bytes 7688 | tf_op jit(solution)/shard_map/ppermute | solution.py:31
  177.0 5.2 %collective-permute-start.13 = (f32[5,32,1]{2,1,0:T(8,128)S(1)}, f32[5,32,1]{2,1,0:T(8,128)S(1)}, u32[]{:S(2)}, u32[]{:S(2)}) collective-permute-start(f32[5,32,1]{2,1,0:T(8,128)S(1)} %get-tuple-element.47), channel_id=1, source_target_pairs={{0,1},{1,0},{2,3},{3,2},{4,5},{5,4},{6,7},{7,6},{8,9},{9,8},{10,11... | collective-permute-start | bytes 1928 | tf_op jit(solution)/shard_map/ppermute | solution.py:28
  178.6 5.4 %collective-permute-start.12 = (f32[5,32,1]{2,1,0:T(8,128)S(1)}, f32[5,32,1]{2,1,0:T(8,128)S(1)}, u32[]{:S(2)}, u32[]{:S(2)}) collective-permute-start(f32[5,32,1]{2,1,0:T(8,128)S(1)} %get-tuple-element.46), channel_id=1, source_target_pairs={{1,0},{0,1},{3,2},{2,3},{5,4},{4,5},{7,6},{6,7},{9,8},{8,9},{11,10... | collective-permute-start | bytes 1928 | tf_op jit(solution)/shard_map/ppermute | solution.py:31
where the time goes:
time: 209 us; the launch traced here: 208 us
  blocking collectives  60 us (29%)
  other arithmetic  45.3 us (22%)
  local copies, waits for them, and re-layouts  38.1 us (18%)
  starting transfers between devices  35.1 us (17%)
  waiting for transfers between devices  26 us (12%)
  matrix products  2.11 us (1%)
    psum x2, blocking collectives, ocean_step(): divergence = lax.psum(partial_div, 'trc')  44.3 us
    mul x4, other arithmetic, face_flux(): return courant * jnp.where(courant >= 0, upwind_pos, upwind_neg)  18.3 us
    ppermute x8, waiting for transfers between devices, padded(): lax.ppermute(lax.slice_in_dim(block, block.shape[dim] - width, None, axis...  16.8 us
    all_gather x1, blocking collectives, body(): lax.all_gather(jnp.stack([east_start, north_start]), 'trc', axis=1, tiled...  15.7 us
    ppermute x8, starting transfers between devices, padded(): lax.ppermute(lax.slice_in_dim(block, block.shape[dim] - width, None, axis...  13.9 us
    ppermute x8, starting transfers between devices, padded(): lax.ppermute(lax.slice_in_dim(block, 0, width, axis=dim), axis, backward)  9.21 us
    ppermute x8, waiting for transfers between devices, padded(): lax.ppermute(lax.slice_in_dim(block, 0, width, axis=dim), axis, backward)  6.48 us
    concatenate x3, other arithmetic, padded(): block = jnp.concatenate([low, block, high], axis=dim)  6.44 us
  transfers between devices with their start and end apart: 19, of which 8 were waited for; matrix products, arithmetic and copies ran while one was open for 19% of the time, Pallas kernels for 0%

commit v1 on v0

--- a/solution.py
+++ b/solution.py
@@ -187,7 +187,12 @@
         zonal_flow_value, meridional_flow_value, free_top_height = ocean_step(
             zonal_flow_value, meridional_flow_value, free_top_height, wet_own, coriolis
         )
-    velocity = lax.all_gather(jnp.stack([east_start, north_start]), "trc", axis=1, tiled=True)
+    velocity = jnp.concatenate(
+        lax.all_to_all(
+            jnp.stack([jnp.stack([east_start, north_start])] * lax.axis_size("trc")), "trc", 0, 0
+        ),
+        axis=1,
+    )
     flow = jnp.concatenate([velocity, wet_all[None]], 0)
     flow_ext = widen_flow(flow, 4)
     first = transport(

time: 209 us -> 213 us (1.019)
  blocking collectives: 60 us -> 44.4 us
  waiting for transfers between devices: 26 us -> 33.5 us
  starting transfers between devices: 35.1 us -> 42.1 us
  other arithmetic: 45.3 us -> 47.7 us
  local copies, waits for them, and re-layouts: 38.1 us -> 40.3 us
    all_gather x1 -> x0, blocking collectives: 15.7 us -> none  [body(): lax.all_gather(jnp.stack([east_start, north_start]), 'trc', axis=1, tiled...]
    all_to_all x0 -> x1, starting transfers between devices: none -> 6.35 us  [body(): lax.all_to_all(jnp.stack([jnp.stack([east_start, north_start])] * lax.axi...]
    ppermute x8, waiting for transfers between devices: 6.48 us -> 11.4 us  [padded(): lax.ppermute(lax.slice_in_dim(block, 0, width, axis=dim), axis, backward)]
    mul x4, other arithmetic: 18.3 us -> 22.8 us  [face_flux(): return courant * jnp.where(courant >= 0, upwind_pos, upwind_neg)]
    ppermute x8, waiting for transfers between devices: 16.8 us -> 19.4 us  [padded(): lax.ppermute(lax.slice_in_dim(block, block.shape[dim] - width, None, axis...]
  transfers between devices with their start and end apart: 19 -> 20, of which waited for: 8 -> 9; matrix products, arithmetic and copies ran while one was open for 19% -> 11% of each run, Pallas kernels for 0% -> 0%
where the time goes in v1:
time: 213 us; the launch traced here: 211 us
  other arithmetic  47.7 us (22%)
  blocking collectives  44.4 us (21%)
  starting transfers between devices  42.1 us (20%)
  local copies, waits for them, and re-layouts  40.3 us (19%)
  waiting for transfers between devices  33.5 us (16%)
    psum x2, blocking collectives, ocean_step(): divergence = lax.psum(partial_div, 'trc')  44.4 us
    mul x4, other arithmetic, face_flux(): return courant * jnp.where(courant >= 0, upwind_pos, upwind_neg)  22.8 us
    ppermute x8, waiting for transfers between devices, padded(): lax.ppermute(lax.slice_in_dim(block, block.shape[dim] - width, None, axis...  19.4 us
    ppermute x8, starting transfers between devices, padded(): lax.ppermute(lax.slice_in_dim(block, block.shape[dim] - width, None, axis...  14.4 us
    ppermute x8, waiting for transfers between devices, padded(): lax.ppermute(lax.slice_in_dim(block, 0, width, axis=dim), axis, backward)  11.4 us
    ppermute x8, starting transfers between devices, padded(): lax.ppermute(lax.slice_in_dim(block, 0, width, axis=dim), axis, backward)  9.35 us
    mul x4, local copies, waits for them, and re-layouts, face_flux(): 0.5 * (1.0 - courant) * limited_slope(after - center, center - before)  7.63 us
    sub x2, other arithmetic, transport(): field[..., rows, cols] - (flux_x[..., 1:] - flux_x[..., :-1])  6.68 us
  transfers between devices with their start and end apart: 20, of which 9 were waited for; matrix products, arithmetic and copies ran while one was open for 11% of the time, Pallas kernels for 0%

profile of v1, /device:TPU:0, one launch (start us, length us, event | category | flops | bytes accessed | tf_op | source)
XLA Modules:
  0.0 211.4 jit_solution(776296008972280988)
XLA Ops:
  3.0 6.3 %all-to-all-start = ((f32[4,2,2,32,128]{4,3,2,1,0:T(8,128)}), f32[4,2,2,32,128]{4,3,2,1,0:T(8,128)S(1)}, u32[]{:S(2)}, u32[]{:S(2)}) async-start(f32[4,2,2,32,128]{4,3,2,1,0:T(8,128)} %stack.19), calls=%async_computation | async-start | bytes 524288 | tf_op jit(solution)/shard_map/all_to_all | solution.py:191
  10.4 1.3 collective-permute-start.1
  11.8 3.0 %collective-permute-start = (f32[8,8,4,128]{3,1,2,0:T(8,128)S(1)}, f32[8,8,4,128]{3,1,2,0:T(8,128)S(1)}, u32[]{:S(2)}, u32[]{:S(2)}) collective-permute-start(f32[8,8,4,128]{3,1,2,0:T(8,128)S(1)} %copy.139), channel_id=1, source_target_pairs={{0,2},{2,4},{4,6},{1,3},{3,5},{5,7},{8,10},{10,12},{12,14},{9,11},... | collective-permute-start | bytes 393224 | tf_op jit(solution)/shard_map/ppermute | solution.py:28
  14.8 3.7 %copy.111 = f32[8,8,32,128]{2,1,3,0:T(8,128)} copy(f32[8,8,32,128]{3,2,1,0:T(8,128)} %param.9) | data formatting | bytes 2097152 | tf_op args[0]
  18.5 2.7 %copy.112 = f32[8,8,4,128]{2,1,3,0:T(8,128)} copy(f32[8,8,4,128]{3,1,2,0:T(8,128)S(1)} %collective-permute-done.1) | data formatting | bytes 262144 | tf_op jit(solution)/shard_map/ppermute | solution.py:31
  21.2 2.8 %copy.110 = f32[8,8,4,128]{2,1,3,0:T(8,128)} copy(f32[8,8,4,128]{3,1,2,0:T(8,128)S(1)} %collective-permute-done) | data formatting | bytes 262144 | tf_op jit(solution)/shard_map/ppermute | solution.py:28
  24.2 1.3 collective-permute-start.5
  25.5 3.6 %collective-permute-start.4 = (f32[3,8,4,128]{3,1,2,0:T(8,128)S(1)}, f32[3,8,4,128]{3,1,2,0:T(8,128)S(1)}, u32[]{:S(2)}, u32[]{:S(2)}) collective-permute-start(f32[3,8,4,128]{3,1,2,0:T(8,128)S(1)} %get-tuple-element.25), channel_id=1, source_target_pairs={{0,2},{2,4},{4,6},{1,3},{3,5},{5,7},{8,10},{10,12},{12,14},{9,11},... | collective-permute-start | bytes 147464 | tf_op jit(solution)/shard_map/ppermute | solution.py:28
  29.2 1.6 pad_maximum_fusion.5
  30.7 1.6 collective-permute-start.3
  33.1 1.6 collective-permute-start.7
  36.4 2.8 %collective-permute-done.2 = f32[8,8,40,4]{2,1,3,0:T(8,128)S(1)} collective-permute-done((f32[8,8,40,4]{2,1,3,0:T(8,128)S(1)}, f32[8,8,40,4]{2,1,3,0:T(8,128)S(1)}, u32[]{:S(2)}, u32[]{:S(2)}) %collective-permute-start.2) | collective-permute-done | bytes 40992 | tf_op jit(solution)/shard_map/ppermute | solution.py:28
  39.2 3.9 %pad_maximum_fusion = f32[8,8,40,136]{2,1,3,0:T(8,128)} fusion(f32[8,8,40,4]{2,1,3,0:T(8,128)S(1)} %collective-permute-done.3, f32[8,8,4,128]{2,1,3,0:T(8,128)S(1)} %copy-done.2, f32[8,8,32,128]{2,1,3,0:T(8,128)S(1)} %copy-done.1, f32[8,8,4,128]{2,1,3,0:T(8,128)S(1)} %copy-done.3, f32[8,8,40,4]{2,1,3,0:T(8,128)S(1)} %collective-permute-done.2), kind=kLoop, calls=%fused_computation.8 | loop fusion | flops 1392640 | bytes 2785280 | tf_op jit(solution)/shard_map/concatenate | solution.py:32
  43.1 6.6 %collective-permute-done.7 = f32[3,8,40,4]{3,1,2,0:T(8,128)S(1)} collective-permute-done((f32[3,8,40,4]{3,1,2,0:T(8,128)S(1)}, f32[3,8,40,4]{3,1,2,0:T(8,128)S(1)}, u32[]{:S(2)}, u32[]{:S(2)}) %collective-permute-start.7) | collective-permute-done | bytes 15392 | tf_op jit(solution)/shard_map/ppermute | solution.py:31
  49.7 10.5 %collective-permute-done.6 = f32[3,8,40,4]{3,1,2,0:T(8,128)S(1)} collective-permute-done((f32[3,8,40,4]{3,1,2,0:T(8,128)S(1)}, f32[3,8,40,4]{3,1,2,0:T(8,128)S(1)}, u32[]{:S(2)}, u32[]{:S(2)}) %collective-permute-start.6) | collective-permute-done | bytes 15392 | tf_op jit(solution)/shard_map/ppermute | solution.py:28
  70.7 1.4 copy.122
  72.1 2.1 %copy.121 = f32[8,37,132]{1,0,2:T(8,128)} copy(f32[8,37,132]{2,0,1:T(8,128)} %get-tuple-element.27) | data formatting | bytes 312576 | tf_op jit(solution)/shard_map/mul | solution.py:45
  75.3 1.4 copy.118
  76.7 1.4 copy.117
  78.1 1.3 copy.116
  79.4 1.9 copy.130
  81.3 2.0 copy.129
  83.3 1.7 copy.128
  86.1 2.2 %copy.125 = f32[8,32,129]{1,0,2:T(8,128)} copy(f32[8,32,129]{2,0,1:T(8,128)} %get-tuple-element.31) | data formatting | bytes 264192 | tf_op jit(solution)/shard_map/mul | solution.py:45
  89.4 9.0 %fusion.12 = f32[8,8,37,132]{2,1,3,0:T(8,128)S(1)} fusion(f32[8,8,40,136]{2,1,3,0:T(8,128)} %pad_maximum_fusion, f32[8,37,132]{1,0,2:T(8,128)S(1)} %copy.122, f32[8,37,132]{1,0,2:T(8,128)} %copy.121, f32[8,37,132]{1,0,2:T(8,128)S(1)} %copy.119, pred[8,37,132]{1,0,2:T(8,128)(4,1)} %copy.120), kind=kLoop, calls=%fused_computation.26 | loop fusion | flops 8126976 | bytes 6759456 | tf_op jit(solution)/shard_map/mul | solution.py:47
  98.4 4.9 %fusion.4 = f32[8,8,36,133]{2,1,3,0:T(8,128)S(1)} fusion(f32[8,8,40,136]{2,1,3,0:T(8,128)S(1)} %bitcast.71, f32[8,36,133]{1,0,2:T(8,128)S(1)} %copy.118, f32[8,36,133]{1,0,2:T(8,128)S(1)} %copy.117, f32[8,36,133]{1,0,2:T(8,128)S(1)} %copy.115, pred[8,36,133]{1,0,2:T(8,128)(4,1)S(1)} %copy.116), kind=kLoop, calls=%fused_computation.13 | loop fusion | flops 7967232 | bytes 6626592 | tf_op jit(solution)/shard_map/mul | solution.py:47
  103.3 2.9 %fusion.16 = f32[8,8,36,132]{2,1,3,0:T(8,128)S(1)} fusion(f32[8,8,37,132]{2,1,3,0:T(8,128)S(1)} %fusion.12, f32[8,8,36,133]{2,1,3,0:T(8,128)S(1)} %fusion.4, f32[8,8,40,136]{2,1,3,0:T(8,128)S(1)} %bitcast.71), kind=kLoop, calls=%fused_computation.31 | loop fusion | flops 1216512 | bytes 7299072 | tf_op jit(solution)/shard_map/sub | solution.py:75
  106.3 4.2 %fusion.30 = f32[8,8,33,128]{2,1,3,0:T(8,128)S(1)} fusion(f32[8,8,36,132]{2,1,3,0:T(8,128)S(1)} %fusion.16, f32[8,33,128]{1,0,2:T(8,128)S(1)} %copy-done.8, f32[8,33,128]{1,0,2:T(8,128)S(1)} %copy-done.9, f32[8,33,128]{1,0,2:T(8,128)S(1)} %copy-done.7, pred[8,33,128]{1,0,2:T(8,128)(4,1)S(1)} %copy-done.13), kind=kLoop, calls=%fused_computation.56 | loop fusion | flops 7028736 | bytes 5846016 | tf_op jit(solution)/shard_map/mul | solution.py:47
  110.6 4.7 %fusion.22 = f32[8,8,32,129]{2,1,3,0:T(8,128)S(1)} fusion(f32[8,8,36,132]{2,1,3,0:T(8,128)S(1)} %fusion.16, f32[8,32,129]{1,0,2:T(8,128)S(1)} %copy-done.5, f32[8,32,129]{1,0,2:T(8,128)S(1)} %copy-done.6, f32[8,32,129]{1,0,2:T(8,128)S(1)} %copy-done.4, pred[8,32,129]{1,0,2:T(8,128)(4,1)S(1)} %copy-done.12), kind=kLoop, calls=%fused_computation.43 | loop fusion | flops 6868992 | bytes 5713152 | tf_op jit(solution)/shard_map/mul | solution.py:47
  115.3 3.8 %fusion.34 = f32[8,8,32,128]{2,1,3,0:T(8,128)} fusion(f32[8,8,33,128]{2,1,3,0:T(8,128)S(1)} %fusion.30, f32[8,8,32,129]{2,1,3,0:T(8,128)S(1)} %fusion.22, f32[8,8,36,132]{2,1,3,0:T(8,128)S(1)} %fusion.16), kind=kLoop, calls=%fused_computation.61 | loop fusion | flops 1048576 | bytes 6291456 | tf_op jit(solution)/shard_map/sub | solution.py:75
  119.1 3.9 %copy.131 = f32[8,8,32,128]{3,1,0,2:T(8,128)} copy(f32[8,8,32,128]{2,1,3,0:T(8,128)} %fusion.34) | data formatting | bytes 2097152 | tf_op jit(solution)/shard_map/sub | solution.py:75
  123.0 5.1 %all-to-all-start.1 = ((f32[8,8,32,128]{3,1,0,2:T(8,128)}), f32[8,8,32,128]{3,1,0,2:T(8,128)S(1)}, u32[]{:S(2)}, u32[]{:S(2)}) async-start(f32[8,8,32,128]{3,1,0,2:T(8,128)} %copy.131), calls=%async_computation.1 | async-start | bytes 2097152 | tf_op jit(solution)/shard_map/all_to_all | solution.py:204
  128.1 2.2 %collective-permute-start.11 = (f32[5,1,128]{2,1,0:T(1,128)S(1)}, f32[5,1,128]{2,1,0:T(1,128)S(1)}, u32[]{:S(2)}, u32[]{:S(2)}) collective-permute-start(f32[5,1,128]{2,1,0:T(1,128)S(1)} %get-tuple-element.50), channel_id=1, source_target_pairs={{0,2},{2,4},{4,6},{1,3},{3,5},{5,7},{8,10},{10,12},{12,14},{9,11},... | collective-permute-start | bytes 7688 | tf_op jit(solution)/shard_map/ppermute | solution.py:28
  130.4 1.3 collective-permute-start.10
  131.8 1.6 collective-permute-start.9
  134.0 3.0 %collective-permute-done.9 = f32[5,32,1]{2,1,0:T(8,128)S(1)} collective-permute-done((f32[5,32,1]{2,1,0:T(8,128)S(1)}, f32[5,32,1]{2,1,0:T(8,128)S(1)}, u32[]{:S(2)}, u32[]{:S(2)}) %collective-permute-start.9) | collective-permute-done | bytes 672 | tf_op jit(solution)/shard_map/ppermute | solution.py:28
  137.0 1.8 collective-permute-done.8
  138.9 24.3 %psum.14 = f32[32,128]{1,0:T(8,128)S(1)} all-reduce(f32[32,128]{1,0:T(8,128)S(1)} %multiply_reduce_fusion.1), channel_id=1, replica_groups=mesh['trc'=4,'lat'=4,'lon'=2] {'trc'}, use_global_device_ids=true, to_apply=%region_2.0 | all-reduce | flops 4096 | bytes 32768 | tf_op jit(solution)/shard_map/psum | solution.py:135
  165.0 3.4 %all-to-all-start.3 = ((f32[8,8,128]{2,1,0:T(8,128)}), f32[8,8,128]{2,1,0:T(8,128)S(1)}, u32[]{:S(2)}, u32[]{:S(2)}) async-start(f32[8,8,128]{2,1,0:T(8,128)} %get-tuple-element.35), calls=%async_computation.3 | async-start | bytes 65536 | tf_op jit(solution)/shard_map/all_to_all | solution.py:216
  168.4 1.3 fusion.38
  169.7 1.6 copy.133
  171.3 2.7 %all-to-all-done.3 = f32[8,8,128]{2,1,0:T(8,128)S(1)} async-done(((f32[8,8,128]{2,1,0:T(8,128)}), f32[8,8,128]{2,1,0:T(8,128)S(1)}, u32[]{:S(2)}, u32[]{:S(2)}) %all-to-all-start.3) | async-done | bytes 32800 | tf_op jit(solution)/shard_map/all_to_all | solution.py:216
  174.0 3.5 %all-to-all-start.2 = ((f32[32,8,8,128]{3,2,1,0:T(8,128)}), f32[32,8,8,128]{3,2,1,0:T(8,128)S(1)}, u32[]{:S(2)}, u32[]{:S(2)}) async-start(f32[32,8,8,128]{3,2,1,0:T(8,128)} %copy.133), calls=%async_computation.2 | async-start | bytes 2097152 | tf_op jit(solution)/shard_map/all_to_all | solution.py:213
  178.8 1.3 collective-permute-start.14
  180.2 1.6 collective-permute-start.13
  182.3 3.1 %collective-permute-done.13 = f32[5,32,1]{2,1,0:T(8,128)S(1)} collective-permute-done((f32[5,32,1]{2,1,0:T(8,128)S(1)}, f32[5,32,1]{2,1,0:T(8,128)S(1)}, u32[]{:S(2)}, u32[]{:S(2)}) %collective-permute-start.13) | collective-permute-done | bytes 672 | tf_op jit(solution)/shard_map/ppermute | solution.py:28
  185.5 1.8 collective-permute-done.12
  187.3 20.2 %psum.15 = f32[32,128]{1,0:T(8,128)S(1)} all-reduce(f32[32,128]{1,0:T(8,128)S(1)} %multiply_reduce_fusion), channel_id=1, replica_groups=mesh['trc'=4,'lat'=4,'lon'=2] {'trc'}, use_global_device_ids=true, to_apply=%region_4.5 | all-reduce | flops 4096 | bytes 32768 | tf_op jit(solution)/shard_map/psum | solution.py:135
  (114 shorter events, 28.5 us)
Async XLA Ops:
  0.6 167.7 %copy-start = (f32[32,32]{1,0:T(8,128)S(1)}, f32[32,32]{1,0:T(8,128)}, u32[]{:S(2)}) copy-start(f32[32,32]{1,0:T(8,128)} %param.15) | copy-start | bytes 12292
  0.6 17.8 %copy-start.15 = (s32[32,128]{1,0:T(8,128)S(1)}, s32[32,128]{1,0:T(8,128)}, u32[]{:S(2)}) copy-start(s32[32,128]{1,0:T(8,128)} %param.14) | copy-start | bytes 49156
  3.0 21.0 %all-to-all-start = ((f32[4,2,2,32,128]{4,3,2,1,0:T(8,128)}), f32[4,2,2,32,128]{4,3,2,1,0:T(8,128)S(1)}, u32[]{:S(2)}, u32[]{:S(2)}) async-start(f32[4,2,2,32,128]{4,3,2,1,0:T(8,128)} %stack.19), calls=%async_computation | async-start | bytes 524288 | tf_op jit(solution)/shard_map/all_to_all | solution.py:191
  10.4 8.1 %collective-permute-start.1 = (f32[8,8,4,128]{3,1,2,0:T(8,128)S(1)}, f32[8,8,4,128]{3,1,2,0:T(8,128)S(1)}, u32[]{:S(2)}, u32[]{:S(2)}) collective-permute-start(f32[8,8,4,128]{3,1,2,0:T(8,128)S(1)} %copy.140), channel_id=1, source_target_pairs={{2,0},{4,2},{6,4},{3,1},{5,3},{7,5},{10,8},{12,10},{14,12},{11,9},... | collective-permute-start | bytes 393224 | tf_op jit(solution)/shard_map/ppermute | solution.py:31
  11.8 9.5 %collective-permute-start = (f32[8,8,4,128]{3,1,2,0:T(8,128)S(1)}, f32[8,8,4,128]{3,1,2,0:T(8,128)S(1)}, u32[]{:S(2)}, u32[]{:S(2)}) collective-permute-start(f32[8,8,4,128]{3,1,2,0:T(8,128)S(1)} %copy.139), channel_id=1, source_target_pairs={{0,2},{2,4},{4,6},{1,3},{3,5},{5,7},{8,10},{10,12},{12,14},{9,11},... | collective-permute-start | bytes 393224 | tf_op jit(solution)/shard_map/ppermute | solution.py:28
  24.2 8.6 %collective-permute-start.5 = (f32[3,8,4,128]{3,1,2,0:T(8,128)S(1)}, f32[3,8,4,128]{3,1,2,0:T(8,128)S(1)}, u32[]{:S(2)}, u32[]{:S(2)}) collective-permute-start(f32[3,8,4,128]{3,1,2,0:T(8,128)S(1)} %get-tuple-element.26), channel_id=1, source_target_pairs={{2,0},{4,2},{6,4},{3,1},{5,3},{7,5},{10,8},{12,10},{14,12},{11,9},... | collective-permute-start | bytes 147464 | tf_op jit(solution)/shard_map/ppermute | solution.py:31
  25.5 7.3 %collective-permute-start.4 = (f32[3,8,4,128]{3,1,2,0:T(8,128)S(1)}, f32[3,8,4,128]{3,1,2,0:T(8,128)S(1)}, u32[]{:S(2)}, u32[]{:S(2)}) collective-permute-start(f32[3,8,4,128]{3,1,2,0:T(8,128)S(1)} %get-tuple-element.25), channel_id=1, source_target_pairs={{0,2},{2,4},{4,6},{1,3},{3,5},{5,7},{8,10},{10,12},{12,14},{9,11},... | collective-permute-start | bytes 147464 | tf_op jit(solution)/shard_map/ppermute | solution.py:28
  29.1 10.1 %copy-start.1 = (f32[8,8,32,128]{2,1,3,0:T(8,128)S(1)}, f32[8,8,32,128]{2,1,3,0:T(8,128)}, u32[]{:S(2)}) copy-start(f32[8,8,32,128]{2,1,3,0:T(8,128)} %copy.111) | copy-start | bytes 3145732
  29.2 10.1 %copy-start.2 = (f32[8,8,4,128]{2,1,3,0:T(8,128)S(1)}, f32[8,8,4,128]{2,1,3,0:T(8,128)}, u32[]{:S(2)}) copy-start(f32[8,8,4,128]{2,1,3,0:T(8,128)} %copy.112) | copy-start | bytes 393220
  29.2 10.1 %copy-start.3 = (f32[8,8,4,128]{2,1,3,0:T(8,128)S(1)}, f32[8,8,4,128]{2,1,3,0:T(8,128)}, u32[]{:S(2)}) copy-start(f32[8,8,4,128]{2,1,3,0:T(8,128)} %copy.110) | copy-start | bytes 393220
  30.7 5.7 %collective-permute-start.3 = (f32[8,8,40,4]{2,1,3,0:T(8,128)S(1)}, f32[8,8,40,4]{2,1,3,0:T(8,128)S(1)}, u32[]{:S(2)}, u32[]{:S(2)}) collective-permute-start(f32[8,8,40,4]{2,1,3,0:T(8,128)S(1)} %get-tuple-element.14), channel_id=1, source_target_pairs={{1,0},{0,1},{3,2},{2,3},{5,4},{4,5},{7,6},{6,7},{9,8},{8,9},{11,10... | collective-permute-start | bytes 122888 | tf_op jit(solution)/shard_map/ppermute | solution.py:31
  32.3 6.9 %collective-permute-start.2 = (f32[8,8,40,4]{2,1,3,0:T(8,128)S(1)}, f32[8,8,40,4]{2,1,3,0:T(8,128)S(1)}, u32[]{:S(2)}, u32[]{:S(2)}) collective-permute-start(f32[8,8,40,4]{2,1,3,0:T(8,128)S(1)} %get-tuple-element.13), channel_id=1, source_target_pairs={{0,1},{1,0},{2,3},{3,2},{4,5},{5,4},{6,7},{7,6},{8,9},{9,8},{10,11... | collective-permute-start | bytes 122888 | tf_op jit(solution)/shard_map/ppermute | solution.py:28
  33.1 16.7 %collective-permute-start.7 = (f32[3,8,40,4]{3,1,2,0:T(8,128)S(1)}, f32[3,8,40,4]{3,1,2,0:T(8,128)S(1)}, u32[]{:S(2)}, u32[]{:S(2)}) collective-permute-start(f32[3,8,40,4]{3,1,2,0:T(8,128)S(1)} %get-tuple-element.24), channel_id=1, source_target_pairs={{1,0},{0,1},{3,2},{2,3},{5,4},{4,5},{7,6},{6,7},{9,8},{8,9},{11,10... | collective-permute-start | bytes 46088 | tf_op jit(solution)/shard_map/ppermute | solution.py:31
  34.7 25.6 %collective-permute-start.6 = (f32[3,8,40,4]{3,1,2,0:T(8,128)S(1)}, f32[3,8,40,4]{3,1,2,0:T(8,128)S(1)}, u32[]{:S(2)}, u32[]{:S(2)}) collective-permute-start(f32[3,8,40,4]{3,1,2,0:T(8,128)S(1)} %get-tuple-element.23), channel_id=1, source_target_pairs={{0,1},{1,0},{2,3},{3,2},{4,5},{5,4},{6,7},{7,6},{8,9},{9,8},{10,11... | collective-permute-start | bytes 46088 | tf_op jit(solution)/shard_map/ppermute | solution.py:28
  68.7 19.6 %copy-start.14 = (pred[8,32,129]{2,0,1:T(8,128)(4,1)S(1)}, pred[8,32,129]{2,0,1:T(8,128)(4,1)}, u32[]{:S(2)}) copy-start(pred[8,32,129]{2,0,1:T(8,128)(4,1)} %get-tuple-element.5) | copy-start | bytes 99076
  70.7 14.2 %copy-start.10 = (f32[8,32,129]{2,0,1:T(8,128)S(1)}, f32[8,32,129]{2,0,1:T(8,128)}, u32[]{:S(2)}) copy-start(f32[8,32,129]{2,0,1:T(8,128)} %get-tuple-element.32) | copy-start | bytes 396292
  86.1 12.2 %slice-start = ((s8[4456448]{0:T(1024)(128)(4,1)}), s8[262144]{0:T(1024)(128)(4,1)S(1)}, s32[]{:S(2)}) async-start(s8[4456448]{0:T(1024)(128)(4,1)} %bitcast.70), calls=%async_computation.4 | async-start | bytes 524288
  89.4 9.0 %slice-start.1 = ((s8[4456448]{0:T(1024)(128)(4,1)}), s8[4194304]{0:T(1024)(128)(4,1)S(1)}, s32[]{:S(2)}) async-start(s8[4456448]{0:T(1024)(128)(4,1)} %bitcast.70), calls=%async_computation.5 | async-start | bytes 8388608
  103.3 2.9 %copy-start.7 = (f32[8,33,128]{1,0,2:T(8,128)S(1)}, f32[8,33,128]{1,0,2:T(8,128)}, u32[]{:S(2)}) copy-start(f32[8,33,128]{1,0,2:T(8,128)} %copy.127) | copy-start | bytes 405508
  103.3 2.9 %copy-start.8 = (f32[8,33,128]{1,0,2:T(8,128)S(1)}, f32[8,33,128]{1,0,2:T(8,128)}, u32[]{:S(2)}) copy-start(f32[8,33,128]{1,0,2:T(8,128)} %copy.130) | copy-start | bytes 405508
  103.3 2.9 %copy-start.9 = (f32[8,33,128]{1,0,2:T(8,128)S(1)}, f32[8,33,128]{1,0,2:T(8,128)}, u32[]{:S(2)}) copy-start(f32[8,33,128]{1,0,2:T(8,128)} %copy.129) | copy-start | bytes 405508
  103.3 2.9 %copy-start.13 = (pred[8,33,128]{1,0,2:T(8,128)(4,1)S(1)}, pred[8,33,128]{1,0,2:T(8,128)(4,1)}, u32[]{:S(2)}) copy-start(pred[8,33,128]{1,0,2:T(8,128)(4,1)} %copy.128) | copy-start | bytes 101380
  106.2 4.3 %copy-start.4 = (f32[8,32,129]{1,0,2:T(8,128)S(1)}, f32[8,32,129]{1,0,2:T(8,128)}, u32[]{:S(2)}) copy-start(f32[8,32,129]{1,0,2:T(8,128)} %copy.123) | copy-start | bytes 396292
  106.3 4.3 %copy-start.5 = (f32[8,32,129]{1,0,2:T(8,128)S(1)}, f32[8,32,129]{1,0,2:T(8,128)}, u32[]{:S(2)}) copy-start(f32[8,32,129]{1,0,2:T(8,128)} %copy.126) | copy-start | bytes 396292
  106.3 4.3 %copy-start.6 = (f32[8,32,129]{1,0,2:T(8,128)S(1)}, f32[8,32,129]{1,0,2:T(8,128)}, u32[]{:S(2)}) copy-start(f32[8,32,129]{1,0,2:T(8,128)} %copy.125) | copy-start | bytes 396292
  106.3 4.3 %copy-start.12 = (pred[8,32,129]{1,0,2:T(8,128)(4,1)S(1)}, pred[8,32,129]{1,0,2:T(8,128)(4,1)}, u32[]{:S(2)}) copy-start(pred[8,32,129]{1,0,2:T(8,128)(4,1)} %copy.124) | copy-start | bytes 99076
  119.1 9.0 %copy-start.11 = (f32[32,128]{1,0:T(8,128)S(1)}, f32[32,128]{1,0:T(8,128)}, u32[]{:S(2)}) copy-start(f32[32,128]{1,0:T(8,128)} %param.13) | copy-start | bytes 49156
  119.1 44.4 %copy-start.17 = (f32[32]{0:T(128)S(1)}, f32[32]{0:T(128)}, u32[]{:S(2)}) copy-start(f32[32]{0:T(128)} %param.17) | copy-start | bytes 388
  119.1 49.3 %copy-start.18 = (f32[32]{0:T(128)S(1)}, f32[32]{0:T(128)}, u32[]{:S(2)}) copy-start(f32[32]{0:T(128)} %param.16) | copy-start | bytes 388
  123.0 40.4 %all-to-all-start.1 = ((f32[8,8,32,128]{3,1,0,2:T(8,128)}), f32[8,8,32,128]{3,1,0,2:T(8,128)S(1)}, u32[]{:S(2)}, u32[]{:S(2)}) async-start(f32[8,8,32,128]{3,1,0,2:T(8,128)} %copy.131), calls=%async_computation.1 | async-start | bytes 2097152 | tf_op jit(solution)/shard_map/all_to_all | solution.py:204
  128.1 10.6 %collective-permute-start.11 = (f32[5,1,128]{2,1,0:T(1,128)S(1)}, f32[5,1,128]{2,1,0:T(1,128)S(1)}, u32[]{:S(2)}, u32[]{:S(2)}) collective-permute-start(f32[5,1,128]{2,1,0:T(1,128)S(1)} %get-tuple-element.50), channel_id=1, source_target_pairs={{0,2},{2,4},{4,6},{1,3},{3,5},{5,7},{8,10},{10,12},{12,14},{9,11},... | collective-permute-start | bytes 7688 | tf_op jit(solution)/shard_map/ppermute | solution.py:28
  130.4 8.4 %collective-permute-start.10 = (f32[5,1,128]{2,1,0:T(1,128)S(1)}, f32[5,1,128]{2,1,0:T(1,128)S(1)}, u32[]{:S(2)}, u32[]{:S(2)}) collective-permute-start(f32[5,1,128]{2,1,0:T(1,128)S(1)} %get-tuple-element.49), channel_id=1, source_target_pairs={{2,0},{4,2},{6,4},{3,1},{5,3},{7,5},{10,8},{12,10},{14,12},{11,9},... | collective-permute-start | bytes 7688 | tf_op jit(solution)/shard_map/ppermute | solution.py:31
  131.8 5.2 %collective-permute-start.9 = (f32[5,32,1]{2,1,0:T(8,128)S(1)}, f32[5,32,1]{2,1,0:T(8,128)S(1)}, u32[]{:S(2)}, u32[]{:S(2)}) collective-permute-start(f32[5,32,1]{2,1,0:T(8,128)S(1)} %get-tuple-element.48), channel_id=1, source_target_pairs={{0,1},{1,0},{2,3},{3,2},{4,5},{5,4},{6,7},{7,6},{8,9},{9,8},{10,11... | collective-permute-start | bytes 1928 | tf_op jit(solution)/shard_map/ppermute | solution.py:28
  133.3 5.4 %collective-permute-start.8 = (f32[5,32,1]{2,1,0:T(8,128)S(1)}, f32[5,32,1]{2,1,0:T(8,128)S(1)}, u32[]{:S(2)}, u32[]{:S(2)}) collective-permute-start(f32[5,32,1]{2,1,0:T(8,128)S(1)} %get-tuple-element.47), channel_id=1, source_target_pairs={{1,0},{0,1},{3,2},{2,3},{5,4},{4,5},{7,6},{6,7},{9,8},{8,9},{11,10... | collective-permute-start | bytes 1928 | tf_op jit(solution)/shard_map/ppermute | solution.py:31
  165.0 44.7 %copy-start.16 = (f32[2,32,128]{2,1,0:T(8,128)S(1)}, f32[2,32,128]{2,1,0:T(8,128)}, u32[]{:S(2)}) copy-start(f32[2,32,128]{2,1,0:T(8,128)} %param.12) | copy-start | bytes 98308
  165.0 9.0 %all-to-all-start.3 = ((f32[8,8,128]{2,1,0:T(8,128)}), f32[8,8,128]{2,1,0:T(8,128)S(1)}, u32[]{:S(2)}, u32[]{:S(2)}) async-start(f32[8,8,128]{2,1,0:T(8,128)} %get-tuple-element.35), calls=%async_computation.3 | async-start | bytes 65536 | tf_op jit(solution)/shard_map/all_to_all | solution.py:216
  174.0 36.3 %all-to-all-start.2 = ((f32[32,8,8,128]{3,2,1,0:T(8,128)}), f32[32,8,8,128]{3,2,1,0:T(8,128)S(1)}, u32[]{:S(2)}, u32[]{:S(2)}) async-start(f32[32,8,8,128]{3,2,1,0:T(8,128)} %copy.133), calls=%async_computation.2 | async-start | bytes 2097152 | tf_op jit(solution)/shard_map/all_to_all | solution.py:213
  177.5 9.7 %collective-permute-start.15 = (f32[5,1,128]{2,1,0:T(1,128)S(1)}, f32[5,1,128]{2,1,0:T(1,128)S(1)}, u32[]{:S(2)}, u32[]{:S(2)}) collective-permute-start(f32[5,1,128]{2,1,0:T(1,128)S(1)} %get-tuple-element.44), channel_id=1, source_target_pairs={{0,2},{2,4},{4,6},{1,3},{3,5},{5,7},{8,10},{10,12},{12,14},{9,11},... | collective-permute-start | bytes 7688 | tf_op jit(solution)/shard_map/ppermute | solution.py:28
  178.8 8.4 %collective-permute-start.14 = (f32[5,1,128]{2,1,0:T(1,128)S(1)}, f32[5,1,128]{2,1,0:T(1,128)S(1)}, u32[]{:S(2)}, u32[]{:S(2)}) collective-permute-start(f32[5,1,128]{2,1,0:T(1,128)S(1)} %get-tuple-element.43), channel_id=1, source_target_pairs={{2,0},{4,2},{6,4},{3,1},{5,3},{7,5},{10,8},{12,10},{14,12},{11,9},... | collective-permute-start | bytes 7688 | tf_op jit(solution)/shard_map/ppermute | solution.py:31
  180.2 5.2 %collective-permute-start.13 = (f32[5,32,1]{2,1,0:T(8,128)S(1)}, f32[5,32,1]{2,1,0:T(8,128)S(1)}, u32[]{:S(2)}, u32[]{:S(2)}) collective-permute-start(f32[5,32,1]{2,1,0:T(8,128)S(1)} %get-tuple-element.42), channel_id=1, source_target_pairs={{0,1},{1,0},{2,3},{3,2},{4,5},{5,4},{6,7},{7,6},{8,9},{9,8},{10,11... | collective-permute-start | bytes 1928 | tf_op jit(solution)/shard_map/ppermute | solution.py:28
  181.8 5.4 %collective-permute-start.12 = (f32[5,32,1]{2,1,0:T(8,128)S(1)}, f32[5,32,1]{2,1,0:T(8,128)S(1)}, u32[]{:S(2)}, u32[]{:S(2)}) collective-permute-start(f32[5,32,1]{2,1,0:T(8,128)S(1)} %get-tuple-element.41), channel_id=1, source_target_pairs={{1,0},{0,1},{3,2},{2,3},{5,4},{4,5},{7,6},{6,7},{9,8},{8,9},{11,10... | collective-permute-start | bytes 1928 | tf_op jit(solution)/shard_map/ppermute | solution.py:31
